TPU v7x, 512 devices: a whole 4x4x16 slice. The times are simulated.
512 devices in a mesh: dp: 32 (over y, x, core), mp: 16 (over z).
Axes of the slice: x: 4, y: 4, z: 16, core: 2. Of those that a mesh axis runs over, the one named last changes fastest.
Arguments:
- tokens: bfloat16 [32768, 8192], P('dp', 'mp'), may hold values from -6 to 6
- value_weight: bfloat16 [8192, 1024], P('mp'), may hold values from -0.0625 to 0.0625
- down_panels: bfloat16 [256, 8192, 64], P('dp', 'mp'), may hold values from -0.0625 to 0.0625
- up_panels: bfloat16 [256, 64, 1024], P('dp'), may hold values from -0.75 to 0.75
- cotangent: bfloat16 [32768, 1024], P(('dp', 'mp')), may hold values from -6 to 6
- block_adapter: int32 [256], replicated, may hold values from 0 to 255, as said below
- adapter_slot: int32 [256], replicated, may hold values from 0 to 255, as said below
Outputs:
- projected: bfloat16 [32768, 1024], P(('dp', 'mp'))
- grad_tokens: bfloat16 [32768, 8192], P('dp', 'mp')
- grad_down: bfloat16 [256, 8192, 64], P('dp', 'mp')
- grad_up: bfloat16 [256, 64, 1024], P('dp')
Inputs may be any that keep to these rules, and one draw needn't show every extreme that they name: `block_adapter`: the 8 blocks of one index of dp name adapters stored on 8 different owners, the owner of slot s being s // 8. `adapter_slot`: A permutation of the adapters.
All inputs are finite; a program needn't handle non-finite values.
Results may differ from a plain program's by a relative error of at most 0.005.
Values may be sent and summed in bfloat16 or wider, within the bound.
A program may use at most 128 MiB of HBM per device.

v0:
```python
import jax
import jax.numpy as jnp
from jax import lax
from jax.sharding import PartitionSpec as P

RANK = 64
BLOCK_ROWS = 128


def per_device(
    tokens, value_weight, down_panels, up_panels, cotangent, block_adapter, adapter_slot
):
    n_owners = lax.axis_size("dp")
    myself = lax.axis_index("dp")
    n_split = lax.axis_size("mp")
    my_part = lax.axis_index("mp")
    rows, width_dev = tokens.shape
    own_rows, kv_full = cotangent.shape
    kv_part = kv_full // n_split
    stored = down_panels.shape[0]
    blocks = rows // BLOCK_ROWS
    group = min(own_rows, BLOCK_ROWS)
    groups = own_rows // group
    highest = lax.Precision.HIGHEST
    hits = block_adapter[:, None] == jnp.arange(adapter_slot.shape[0], dtype=jnp.int32)[None, :]
    slots_all = jnp.sum(jnp.where(hits, adapter_slot[None, :], 0), axis=1)
    owner_all = (slots_all // stored).reshape(n_owners, blocks)
    local_all = (slots_all % stored).reshape(n_owners, blocks)
    mine = owner_all == myself
    wanted = jnp.sum(jnp.where(mine, local_all, 0), axis=1)
    served = jnp.any(mine, axis=1)
    pick_mask = (wanted[:, None] == jnp.arange(stored, dtype=jnp.int32)[None, :]) & served[:, None]
    pick_bf = pick_mask.astype(jnp.bfloat16)
    my_owner = lax.dynamic_index_in_dim(owner_all, myself, 0, keepdims=False)
    select_mask = my_owner[:, None] == jnp.arange(n_owners, dtype=jnp.int32)[None, :]
    select_bf = select_mask.astype(jnp.bfloat16)
    select_f32 = select_mask.astype(jnp.float32)
    send_a = jnp.einsum(
        "ra,adk->rdk", pick_bf, down_panels, preferred_element_type=jnp.float32
    ).astype(jnp.bfloat16)
    send_b = jnp.einsum(
        "ra,akc->rkc", pick_bf, up_panels, preferred_element_type=jnp.float32
    ).astype(jnp.bfloat16)
    got_a, got_b = (
        lax.all_to_all(send_a, "dp", split_axis=0, concat_axis=0, tiled=True),
        lax.all_to_all(send_b, "dp", split_axis=0, concat_axis=0, tiled=True),
    )
    panel_a = jnp.einsum(
        "bo,odk->bdk", select_bf, got_a, preferred_element_type=jnp.float32
    ).astype(jnp.bfloat16)
    panel_b = jnp.einsum(
        "bo,okc->bkc", select_bf, got_b, preferred_element_type=jnp.float32
    ).astype(jnp.bfloat16)
    token_blocks = tokens.reshape(blocks, BLOCK_ROWS, width_dev)
    partial_value = jnp.dot(tokens, value_weight, preferred_element_type=jnp.float32)
    base = lax.psum_scatter(partial_value, "mp", scatter_dimension=0, tiled=True)
    down_part = jnp.einsum(
        "bnd,bdk->bnk", token_blocks, panel_a, preferred_element_type=jnp.float32
    )
    down = lax.psum(down_part, "mp").astype(jnp.bfloat16)
    first_row = my_part * own_rows
    my_down = lax.dynamic_slice_in_dim(down.reshape(rows, RANK), first_row, own_rows, 0).reshape(
        groups, group, RANK
    )
    group_blocks = (first_row + jnp.arange(groups, dtype=jnp.int32) * group) // BLOCK_ROWS
    my_up = jnp.take(panel_b, group_blocks, axis=0)
    lifted = jnp.einsum("gnk,gkc->gnc", my_down, my_up, preferred_element_type=jnp.float32)
    projected = (base + lifted.reshape(own_rows, kv_full)).astype(jnp.bfloat16)
    cot_all = lax.all_gather(cotangent, "mp", axis=0, tiled=True)
    grad_base = jnp.einsum("nc,dc->nd", cot_all, value_weight, preferred_element_type=jnp.float32)
    cot_blocks = cot_all.reshape(blocks, BLOCK_ROWS, kv_full)
    back = jnp.einsum(
        "bnc,bkc->bnk", cot_blocks, panel_b, preferred_element_type=jnp.float32
    ).astype(jnp.bfloat16)
    through = jnp.einsum("bnk,bdk->bnd", back, panel_a, preferred_element_type=jnp.float32)
    grad_tokens = (grad_base + through.reshape(rows, width_dev)).astype(jnp.bfloat16)
    block_grad_a = jnp.einsum(
        "bnd,bnk->bdk", token_blocks, back, preferred_element_type=jnp.float32
    )
    cot_share = lax.dynamic_slice_in_dim(cot_blocks, my_part * kv_part, kv_part, 2)
    block_grad_b = jnp.einsum("bnk,bnc->bkc", down, cot_share, preferred_element_type=jnp.float32)
    send_ga = jnp.einsum("bo,bdk->odk", select_f32, block_grad_a, precision=highest)
    send_gb = jnp.einsum("bo,bkc->okc", select_f32, block_grad_b, precision=highest)
    recv_ga, recv_gb = (
        lax.all_to_all(send_ga, "dp", split_axis=0, concat_axis=0, tiled=True),
        lax.all_to_all(send_gb, "dp", split_axis=0, concat_axis=0, tiled=True),
    )
    pick_f32 = pick_mask.astype(jnp.float32)
    grad_down = jnp.einsum("ra,rdk->adk", pick_f32, recv_ga, precision=highest).astype(jnp.bfloat16)
    grad_share = jnp.einsum("ra,rkc->akc", pick_f32, recv_gb, precision=highest).astype(
        jnp.bfloat16
    )
    grad_up = lax.all_gather(grad_share, "mp", axis=2, tiled=True)
    return (projected, grad_tokens, grad_down, grad_up)


def solution(mesh):
    placed = (
        P("dp", "mp"),
        P("mp", None),
        P("dp", "mp", None),
        P("dp", None, None),
        P(("dp", "mp"), None),
        P(),
        P(),
    )
    return jax.shard_map(
        per_device,
        mesh=mesh,
        in_specs=placed,
        out_specs=(P(("dp", "mp"), None), P("dp", "mp"), P("dp", "mp", None), P("dp", None, None)),
        check_vma=False,
    )
```

profile of v0, /device:TPU:2, one launch (start us, length us, event | category | flops | bytes accessed | tf_op | source)
XLA Modules:
  0.0 294.6 jit_solution(1035140061272832880)
XLA Ops:
  9.1 1.8 convolution_convert_fusion.1
  11.0 2.5 copy.43
  13.5 9.6 %all-to-all-start = ((bf16[32,512,64]{1,2,0:T(8,128)(2,1)}), bf16[32,512,64]{1,2,0:T(8,128)(2,1)S(1)}, u32[]{:S(2)}, u32[]{:S(2)}) async-start(bf16[32,512,64]{1,2,0:T(8,128)(2,1)} %copy.43), calls=%async_computation.1 | async-start | bytes 4194304 | tf_op jit(solution)/shard_map/all_to_all | solution.py:45
  23.1 27.9 %all-to-all-done = bf16[32,512,64]{1,2,0:T(8,128)(2,1)S(1)} async-done(((bf16[32,512,64]{1,2,0:T(8,128)(2,1)}), bf16[32,512,64]{1,2,0:T(8,128)(2,1)S(1)}, u32[]{:S(2)}, u32[]{:S(2)}) %all-to-all-start) | async-done | bytes 2097184 | tf_op jit(solution)/shard_map/all_to_all | solution.py:45
  51.0 1.2 fusion.10
  53.5 63.4 %all-reduce.1 = bf16[8,128,64]{1,2,0:T(8,128)(2,1)S(1)} all-reduce(f32[8,128,64]{1,2,0:T(8,128)S(1)} %convolution_bitcast_fusion.1), channel_id=1, replica_groups=mesh['dp'=32,'mp'=16] {'mp'}, use_global_device_ids=true, to_apply=%region_4.5 | all-reduce | flops 65536 | bytes 393216 | tf_op jit(solution)/shard_map/psum | solution.py:60
  117.0 1.2 fusion.28
  120.2 14.8 %all_to_all.20 = f32[32,1,4096]{2,1,0:T(1,128)S(1)} all-to-all(f32[32,1,4096]{2,1,0:T(1,128)S(1)} %reshape.88), channel_id=1, replica_groups=mesh['dp'=32,'mp'=16] {'dp'}, dimensions={0} | all-to-all | bytes 1048576 | tf_op jit(solution)/shard_map/all_to_all | solution.py:86
  135.5 1.9 reduce
  139.7 1.3 convolution_convert_fusion
  141.0 4.3 %copy.48 = bf16[32,64,1024]{2,1,0:T(8,128)(2,1)} copy(bf16[32,64,1024]{2,0,1:T(8,128)(2,1)S(1)} %convolution_convert_fusion) | data formatting | bytes 8388608 | tf_op jit(solution)/shard_map/convert_element_type | solution.py:43
  145.3 6.1 %all-to-all-start.1 = ((bf16[32,64,1024]{2,1,0:T(8,128)(2,1)}), bf16[32,64,1024]{2,1,0:T(8,128)(2,1)}, u32[]{:S(2)}, u32[]{:S(2)}) async-start(bf16[32,64,1024]{2,1,0:T(8,128)(2,1)} %copy.48), calls=%async_computation.2 | async-start | bytes 8388608 | tf_op jit(solution)/shard_map/all_to_all | solution.py:46
  151.7 3.2 %fusion.57 = f32[1024,1024]{1,0:T(8,128)} fusion(bf16[1024,512]{1,0:T(8,128)(2,1)S(1)} %copy-done.4, bf16[512,1024]{1,0:T(8,128)(2,1)S(1)} %copy-done.7), kind=kOutput, calls=%fused_computation.66 | convolution fusion | flops 1073741824 | bytes 6291456 | tf_op jit(solution)/shard_map/dot_general | solution.py:55
  154.9 48.0 %all-to-all-done.1 = bf16[32,64,1024]{2,1,0:T(8,128)(2,1)} async-done(((bf16[32,64,1024]{2,1,0:T(8,128)(2,1)}), bf16[32,64,1024]{2,1,0:T(8,128)(2,1)}, u32[]{:S(2)}, u32[]{:S(2)}) %all-to-all-start.1) | async-done | bytes 4194336 | tf_op jit(solution)/shard_map/all_to_all | solution.py:46
  202.8 6.9 %fusion.7 = bf16[8,64,1024]{2,0,1:T(8,128)(2,1)S(1)} fusion(bf16[32,64,1024]{2,1,0:T(8,128)(2,1)} %all-to-all-done.1, s32[8]{0:T(128)S(1)} %fusion.51), kind=kOutput, calls=%fused_computation.10 | convolution fusion | flops 34078976 | bytes 5242912 | tf_op jit(solution)/shard_map/bo,okc->bkc/dot_general | solution.py:51
  210.9 2.1 fusion.18
  213.0 4.4 %copy.53 = f32[32,512,64]{1,2,0:T(8,128)} copy(f32[32,512,64]{1,0,2:T(8,128)S(1)} %fusion.18) | data formatting | bytes 8388608 | tf_op jit(solution)/shard_map/bo,bdk->odk/dot_general | solution.py:82
  217.4 7.0 %all-to-all-start.2 = ((f32[32,512,64]{1,2,0:T(8,128)}), f32[32,512,64]{1,2,0:T(8,128)}, u32[]{:S(2)}, u32[]{:S(2)}) async-start(f32[32,512,64]{1,2,0:T(8,128)} %copy.53), calls=%async_computation.3 | async-start | bytes 8388608 | tf_op jit(solution)/shard_map/all_to_all | solution.py:85
  226.3 2.3 fusion.4
  228.5 3.3 %copy.61 = bf16[8,64,1024]{2,1,0:T(8,128)(2,1)} copy(bf16[8,64,1024]{1,0,2:T(8,128)(2,1)} %all-gather.5.cloned.1.call-done) | data formatting | bytes 2097152
  231.9 44.0 %all-to-all-done.2 = f32[32,512,64]{1,2,0:T(8,128)} async-done(((f32[32,512,64]{1,2,0:T(8,128)}), f32[32,512,64]{1,2,0:T(8,128)}, u32[]{:S(2)}, u32[]{:S(2)}) %all-to-all-start.2) | async-done | bytes 4194336 | tf_op jit(solution)/shard_map/all_to_all | solution.py:85
  275.9 5.8 %fusion.13 = bf16[8,512,64]{1,0,2:T(8,128)(2,1)S(1)} fusion(f32[32,512,64]{1,2,0:T(8,128)} %all-to-all-done.2, s32[32]{0:T(128)S(1)} %fusion.34, pred[32]{0:T(512)(128)(4,1)S(1)} %get-tuple-element.31), kind=kOutput, calls=%fused_computation.13 | convolution fusion | flops 100925952 | bytes 4718752 | tf_op jit(solution)/shard_map/ra,rdk->adk/dot_general | solution.py:89
  282.7 3.5 %reduce-scatter.2.cloned.1.call-done = f32[64,1024]{1,0:T(8,128)} async-done(((f32[1024,1024]{1,0:T(8,128)}), f32[64,1024]{1,0:T(8,128)}) %reduce-scatter.2.cloned.1.call-update) | async-done | bytes 262160 | tf_op jit(solution)/shard_map/reduce_scatter | solution.py:56
  286.2 1.9 fusion.16
  (45 shorter events, 12.3 us)
Async XLA Ops:
  7.2 132.5 %copy-start = (bf16[8,64,1024]{2,1,0:T(8,128)(2,1)S(1)}, bf16[8,64,1024]{2,1,0:T(8,128)(2,1)}, u32[]{:S(2)}) copy-start(bf16[8,64,1024]{2,1,0:T(8,128)(2,1)} %param.10) | copy-start | bytes 3145732
  7.2 109.8 %all-gather.3.cloned.1.call-start = ((), (), s32[]{:S(2)}) async-start(), calls=%async_computation.6 | async-start | bytes 2228224 | tf_op jit(solution)/shard_map/all_gather | solution.py:69
  13.5 37.6 %all-to-all-start = ((bf16[32,512,64]{1,2,0:T(8,128)(2,1)}), bf16[32,512,64]{1,2,0:T(8,128)(2,1)S(1)}, u32[]{:S(2)}, u32[]{:S(2)}) async-start(bf16[32,512,64]{1,2,0:T(8,128)(2,1)} %copy.43), calls=%async_computation.1 | async-start | bytes 4194304 | tf_op jit(solution)/shard_map/all_to_all | solution.py:45
  23.1 205.5 %all-gather.5.cloned.1.call-start = ((), (), s32[]{:S(2)}) async-start(), calls=%async_computation.7 | async-start | bytes 2228224 | tf_op jit(solution)/shard_map/all_gather | solution.py:93
  51.0 2.0 copy-start.3
  52.3 0.8 copy-start.1
  145.3 6.4 %copy-start.4 = (bf16[1024,512]{1,0:T(8,128)(2,1)S(1)}, bf16[1024,512]{1,0:T(8,128)(2,1)}, u32[]{:S(2)}) copy-start(bf16[1024,512]{1,0:T(8,128)(2,1)} %param.7) | copy-start | bytes 3145732
  145.3 6.4 %copy-start.7 = (bf16[512,1024]{1,0:T(8,128)(2,1)S(1)}, bf16[512,1024]{1,0:T(8,128)(2,1)}, u32[]{:S(2)}) copy-start(bf16[512,1024]{1,0:T(8,128)(2,1)} %param.8) | copy-start | bytes 3145732
  145.3 57.5 %all-to-all-start.1 = ((bf16[32,64,1024]{2,1,0:T(8,128)(2,1)}), bf16[32,64,1024]{2,1,0:T(8,128)(2,1)}, u32[]{:S(2)}, u32[]{:S(2)}) async-start(bf16[32,64,1024]{2,1,0:T(8,128)(2,1)} %copy.48), calls=%async_computation.2 | async-start | bytes 8388608 | tf_op jit(solution)/shard_map/all_to_all | solution.py:46
  151.4 134.8 %reduce-scatter.2.cloned.1.call-start = ((), (), s32[]{:S(2)}) async-start(), calls=%async_computation.5 | async-start | bytes 4456448 | tf_op jit(solution)/shard_map/reduce_scatter | solution.py:56
  202.8 6.9 %copy-start.5 = (bf16[1024,1024]{1,0:T(8,128)(2,1)S(1)}, bf16[1024,1024]{1,0:T(8,128)(2,1)}, u32[]{:S(2)}) copy-start(bf16[1024,1024]{1,0:T(8,128)(2,1)} %all-gather.3.cloned.1.call-done) | copy-start | bytes 6291460
  217.4 7.4 %copy-start.2 = (bf16[8,512,64]{1,0,2:T(8,128)(2,1)S(1)}, bf16[8,512,64]{1,0,2:T(8,128)(2,1)}, u32[]{:S(2)}) copy-start(bf16[8,512,64]{1,0,2:T(8,128)(2,1)} %copy-done.1) | copy-start | bytes 1572868
  217.4 58.4 %all-to-all-start.2 = ((f32[32,512,64]{1,2,0:T(8,128)}), f32[32,512,64]{1,2,0:T(8,128)}, u32[]{:S(2)}, u32[]{:S(2)}) async-start(f32[32,512,64]{1,2,0:T(8,128)} %copy.53), calls=%async_computation.3 | async-start | bytes 8388608 | tf_op jit(solution)/shard_map/all_to_all | solution.py:85
  224.4 1.6 copy-start.6
  224.4 1.8 copy-start.8
Sparse Core Ops, SparseCore 0:
  10.1 78.1 all-gather.2
  139.8 66.9 all-gather.4
  209.6 76.5 reduce-scatter.1
where the time goes:
time: 295 us
  waiting for transfers between devices  124 us (42%)
  blocking collectives  78.2 us (27%)
  matrix products  31.6 us (11%)
  starting transfers between devices  23 us (8%)
  local copies, waits for them, and re-layouts  20.3 us (7%)
  between operations  14 us (5%)
  other arithmetic  3.37 us (1%)
    psum x1, blocking collectives, per_device(): down = lax.psum(down_part, 'mp').astype(jnp.bfloat16)  63.4 us
    all_to_all x1, waiting for transfers between devices, per_device(): lax.all_to_all(send_b, 'dp', split_axis=0, concat_axis=0, tiled=True)  48 us
    all_to_all x1, waiting for transfers between devices, per_device(): lax.all_to_all(send_ga, 'dp', split_axis=0, concat_axis=0, tiled=True)  44 us
    all_to_all x1, waiting for transfers between devices, per_device(): lax.all_to_all(send_a, 'dp', split_axis=0, concat_axis=0, tiled=True)  27.9 us
    all_to_all x1, blocking collectives, per_device(): lax.all_to_all(send_gb, 'dp', split_axis=0, concat_axis=0, tiled=True)  14.8 us
    all_to_all x1, starting transfers between devices, per_device(): lax.all_to_all(send_a, 'dp', split_axis=0, concat_axis=0, tiled=True)  9.58 us
    unnamed x22, local copies, waits for them, and re-layouts  7.08 us
    all_to_all x1, starting transfers between devices, per_device(): lax.all_to_all(send_ga, 'dp', split_axis=0, concat_axis=0, tiled=True)  6.98 us
  transfers between devices with their start and end apart: 6, of which 4 were waited for; matrix products, arithmetic and copies ran while one was open for 15% of the time, Pallas kernels for 0%

commit v1 on v0

--- a/solution.py
+++ b/solution.py
@@ -57,7 +57,7 @@
     down_part = jnp.einsum(
         "bnd,bdk->bnk", token_blocks, panel_a, preferred_element_type=jnp.float32
     )
-    down = lax.psum(down_part, "mp").astype(jnp.bfloat16)
+    down = jnp.sum(lax.all_gather(down_part, "mp"), axis=0).astype(jnp.bfloat16)
     first_row = my_part * own_rows
     my_down = lax.dynamic_slice_in_dim(down.reshape(rows, RANK), first_row, own_rows, 0).reshape(
         groups, group, RANK

time: 295 us -> 329 us (1.12)
  waiting for transfers between devices: 124 us -> 218 us
  blocking collectives: 78.2 us -> 0 us
  starting transfers between devices: 23 us -> 30.6 us
  local copies, waits for them, and re-layouts: 20.3 us -> 24.3 us
  other arithmetic: 3.37 us -> 6.95 us
  matrix products: 31.6 us -> 34.9 us
    psum x1 -> x0, blocking collectives: 63.4 us -> none  [per_device(): down = lax.psum(down_part, 'mp').astype(jnp.bfloat16)]
    all_gather x1, waiting for transfers between devices: 0.01 us -> 59.6 us  [per_device(): grad_up = lax.all_gather(grad_share, 'mp', axis=2, tiled=True)]
    all_gather x0 -> x1, waiting for transfers between devices: none -> 38.2 us  [per_device(): down = jnp.sum(lax.all_gather(down_part, 'mp'), axis=0).astype(jnp.bfloat16)]
    all_to_all x1 -> x0, blocking collectives: 14.8 us -> none  [per_device(): lax.all_to_all(send_gb, 'dp', split_axis=0, concat_axis=0, tiled=True)]
    all_to_all x0 -> x1, starting transfers between devices: none -> 7.79 us  [per_device(): lax.all_to_all(send_gb, 'dp', split_axis=0, concat_axis=0, tiled=True)]
    all_to_all x1, waiting for transfers between devices: 44 us -> 39.3 us  [per_device(): lax.all_to_all(send_ga, 'dp', split_axis=0, concat_axis=0, tiled=True)]
    all_to_all x0 -> x1, waiting for transfers between devices: none -> 3.74 us  [per_device(): lax.all_to_all(send_gb, 'dp', split_axis=0, concat_axis=0, tiled=True)]
    reduce_scatter x1, waiting for transfers between devices: 3.54 us -> 0.02 us  [per_device(): lax.psum_scatter(partial_value, 'mp', scatter_dimension=0, tiled=True)]
  transfers between devices with their start and end apart: 6 -> 8, of which waited for: 4 -> 6; matrix products, arithmetic and copies ran while one was open for 15% -> 19% of each run, Pallas kernels for 0% -> 0%
where the time goes in v1:
time: 329 us; the launch traced here: 328 us
  waiting for transfers between devices  218 us (66%)
  matrix products  34.9 us (11%)
  starting transfers between devices  30.6 us (9%)
  local copies, waits for them, and re-layouts  24.3 us (7%)
  between operations  14 us (4%)
  other arithmetic  6.95 us (2%)
    all_gather x1, waiting for transfers between devices, per_device(): grad_up = lax.all_gather(grad_share, 'mp', axis=2, tiled=True)  59.6 us
    all_to_all x1, waiting for transfers between devices, per_device(): lax.all_to_all(send_b, 'dp', split_axis=0, concat_axis=0, tiled=True)  48 us
    all_to_all x1, waiting for transfers between devices, per_device(): lax.all_to_all(send_ga, 'dp', split_axis=0, concat_axis=0, tiled=True)  39.3 us
    all_gather x1, waiting for transfers between devices, per_device(): down = jnp.sum(lax.all_gather(down_part, 'mp'), axis=0).astype(jnp.bfloat16)  38.2 us
    all_to_all x1, waiting for transfers between devices, per_device(): lax.all_to_all(send_a, 'dp', split_axis=0, concat_axis=0, tiled=True)  27.9 us
    unnamed x20, local copies, waits for them, and re-layouts  10.1 us
    all_to_all x1, starting transfers between devices, per_device(): lax.all_to_all(send_a, 'dp', split_axis=0, concat_axis=0, tiled=True)  9.58 us
    all_to_all x1, starting transfers between devices, per_device(): lax.all_to_all(send_gb, 'dp', split_axis=0, concat_axis=0, tiled=True)  7.79 us
  transfers between devices with their start and end apart: 8, of which 6 were waited for; matrix products, arithmetic and copies ran while one was open for 19% of the time, Pallas kernels for 0%

profile of v1, /device:TPU:2, one launch (start us, length us, event | category | flops | bytes accessed | tf_op | source)
XLA Modules:
  0.0 328.4 jit_solution(6642053457209111825)
XLA Ops:
  11.0 2.5 copy.61
  13.4 9.6 %all-to-all-start = ((bf16[32,512,64]{1,2,0:T(8,128)(2,1)}), bf16[32,512,64]{1,2,0:T(8,128)(2,1)S(1)}, u32[]{:S(2)}, u32[]{:S(2)}) async-start(bf16[32,512,64]{1,2,0:T(8,128)(2,1)} %copy.61), calls=%async_computation.1 | async-start | bytes 4194304 | tf_op jit(solution)/shard_map/all_to_all | solution.py:45
  23.1 27.9 %all-to-all-done = bf16[32,512,64]{1,2,0:T(8,128)(2,1)S(1)} async-done(((bf16[32,512,64]{1,2,0:T(8,128)(2,1)}), bf16[32,512,64]{1,2,0:T(8,128)(2,1)S(1)}, u32[]{:S(2)}, u32[]{:S(2)}) %all-to-all-start) | async-done | bytes 2097184 | tf_op jit(solution)/shard_map/all_to_all | solution.py:45
  55.6 4.3 %copy.66 = bf16[32,64,1024]{2,1,0:T(8,128)(2,1)} copy(bf16[32,64,1024]{2,0,1:T(8,128)(2,1)S(1)} %convolution_convert_fusion) | data formatting | bytes 8388608 | tf_op jit(solution)/shard_map/convert_element_type | solution.py:43
  59.8 6.9 %all-to-all-start.1 = ((bf16[32,64,1024]{2,1,0:T(8,128)(2,1)}), bf16[32,64,1024]{2,1,0:T(8,128)(2,1)}, u32[]{:S(2)}, u32[]{:S(2)}) async-start(bf16[32,64,1024]{2,1,0:T(8,128)(2,1)} %copy.66), calls=%async_computation.2 | async-start | bytes 8388608 | tf_op jit(solution)/shard_map/all_to_all | solution.py:46
  67.0 3.2 fusion.57
  70.2 48.0 %all-to-all-done.1 = bf16[32,64,1024]{2,1,0:T(8,128)(2,1)} async-done(((bf16[32,64,1024]{2,1,0:T(8,128)(2,1)}), bf16[32,64,1024]{2,1,0:T(8,128)(2,1)}, u32[]{:S(2)}, u32[]{:S(2)}) %all-to-all-start.1) | async-done | bytes 4194336 | tf_op jit(solution)/shard_map/all_to_all | solution.py:46
  118.2 6.7 %fusion.7 = bf16[8,64,1024]{2,0,1:T(8,128)(2,1)S(1)} fusion(bf16[32,64,1024]{2,1,0:T(8,128)(2,1)} %all-to-all-done.1, s32[8]{0:T(128)S(1)} %fusion.51), kind=kOutput, calls=%fused_computation.10 | convolution fusion | flops 34078976 | bytes 5242912 | tf_op jit(solution)/shard_map/bo,okc->bkc/dot_general | solution.py:51
  125.0 2.5 convolution_convert_fusion.3
  127.5 38.2 %all-gather.9.cloned.1.call-done = f32[128,128,64]{1,2,0:T(8,128)} async-done(((f32[8,128,64]{1,2,0:T(8,128)}), f32[128,128,64]{1,2,0:T(8,128)}) %all-gather.9.cloned.1.call-update) | async-done | bytes 4194320 | tf_op jit(solution)/shard_map/all_gather | solution.py:60
  165.7 2.5 reduce_sum.32
  171.8 2.7 reshape.88
  174.4 7.8 %all-to-all-start.3 = ((f32[32,1,4096]{2,1,0:T(1,128)}), f32[32,1,4096]{2,1,0:T(1,128)}, u32[]{:S(2)}, u32[]{:S(2)}) async-start(f32[32,1,4096]{2,1,0:T(1,128)} %reshape.88), calls=%async_computation.4 | async-start | bytes 1048576 | tf_op jit(solution)/shard_map/all_to_all | solution.py:86
  182.5 2.1 fusion.18
  184.6 4.4 %copy.71 = f32[32,512,64]{1,2,0:T(8,128)} copy(f32[32,512,64]{1,0,2:T(8,128)S(1)} %fusion.18) | data formatting | bytes 8388608 | tf_op jit(solution)/shard_map/bo,bdk->odk/dot_general | solution.py:82
  189.0 3.7 %all-to-all-done.3 = f32[32,1,4096]{2,1,0:T(1,128)} async-done(((f32[32,1,4096]{2,1,0:T(1,128)}), f32[32,1,4096]{2,1,0:T(1,128)}, u32[]{:S(2)}, u32[]{:S(2)}) %all-to-all-start.3) | async-done | bytes 524320 | tf_op jit(solution)/shard_map/all_to_all | solution.py:86
  192.8 6.0 %all-to-all-start.2 = ((f32[32,512,64]{1,2,0:T(8,128)}), f32[32,512,64]{1,2,0:T(8,128)}, u32[]{:S(2)}, u32[]{:S(2)}) async-start(f32[32,512,64]{1,2,0:T(8,128)} %copy.71), calls=%async_computation.3 | async-start | bytes 8388608 | tf_op jit(solution)/shard_map/all_to_all | solution.py:85
  199.3 2.9 reduce
  203.7 2.2 convolution_convert_fusion.2
  208.6 2.3 fusion.4
  210.9 39.3 %all-to-all-done.2 = f32[32,512,64]{1,2,0:T(8,128)} async-done(((f32[32,512,64]{1,2,0:T(8,128)}), f32[32,512,64]{1,2,0:T(8,128)}, u32[]{:S(2)}, u32[]{:S(2)}) %all-to-all-start.2) | async-done | bytes 4194336 | tf_op jit(solution)/shard_map/all_to_all | solution.py:85
  250.2 5.8 %fusion.13 = bf16[8,512,64]{1,0,2:T(8,128)(2,1)S(1)} fusion(f32[32,512,64]{1,2,0:T(8,128)} %all-to-all-done.2, s32[32]{0:T(128)S(1)} %fusion.34, pred[32]{0:T(512)(128)(4,1)S(1)} %get-tuple-element.35), kind=kOutput, calls=%fused_computation.13 | convolution fusion | flops 100925952 | bytes 4718752 | tf_op jit(solution)/shard_map/ra,rdk->adk/dot_general | solution.py:89
  258.9 59.6 %all-gather.7.cloned.1.call-done = bf16[8,64,1024]{1,0,2:T(8,128)(2,1)} async-done(((bf16[8,64,64]{1,0,2:T(8,128)(2,1)}), bf16[8,64,1024]{1,0,2:T(8,128)(2,1)}) %all-gather.7.cloned.1.call-update) | async-done | bytes 1048592 | tf_op jit(solution)/shard_map/all_gather | solution.py:93
  318.5 3.3 %copy.79 = bf16[8,64,1024]{2,1,0:T(8,128)(2,1)} copy(bf16[8,64,1024]{1,0,2:T(8,128)(2,1)} %all-gather.7.cloned.1.call-done) | data formatting | bytes 2097152
  (47 shorter events, 19.8 us)
Async XLA Ops:
  7.2 47.1 %copy-start = (bf16[8,64,1024]{2,1,0:T(8,128)(2,1)S(1)}, bf16[8,64,1024]{2,1,0:T(8,128)(2,1)}, u32[]{:S(2)}) copy-start(bf16[8,64,1024]{2,1,0:T(8,128)(2,1)} %param.10) | copy-start | bytes 3145732
  7.2 117.8 %all-gather.5.cloned.1.call-start = ((), (), s32[]{:S(2)}) async-start(), calls=%async_computation.6 | async-start | bytes 2228224 | tf_op jit(solution)/shard_map/all_gather | solution.py:69
  13.4 37.6 %all-to-all-start = ((bf16[32,512,64]{1,2,0:T(8,128)(2,1)}), bf16[32,512,64]{1,2,0:T(8,128)(2,1)S(1)}, u32[]{:S(2)}, u32[]{:S(2)}) async-start(bf16[32,512,64]{1,2,0:T(8,128)(2,1)} %copy.61), calls=%async_computation.1 | async-start | bytes 4194304 | tf_op jit(solution)/shard_map/all_to_all | solution.py:45
  23.0 142.7 %all-gather.9.cloned.1.call-start = ((), (), s32[]{:S(2)}) async-start(), calls=%async_computation.8 | async-start | bytes 4456448 | tf_op jit(solution)/shard_map/all_gather | solution.py:60
  51.0 2.0 copy-start.3
  52.2 0.8 copy-start.1
  59.8 7.2 %copy-start.4 = (bf16[1024,512]{1,0:T(8,128)(2,1)S(1)}, bf16[1024,512]{1,0:T(8,128)(2,1)}, u32[]{:S(2)}) copy-start(bf16[1024,512]{1,0:T(8,128)(2,1)} %param.7) | copy-start | bytes 3145732
  59.8 7.2 %copy-start.6 = (bf16[512,1024]{1,0:T(8,128)(2,1)S(1)}, bf16[512,1024]{1,0:T(8,128)(2,1)}, u32[]{:S(2)}) copy-start(bf16[512,1024]{1,0:T(8,128)(2,1)} %param.8) | copy-start | bytes 3145732
  59.8 58.4 %all-to-all-start.1 = ((bf16[32,64,1024]{2,1,0:T(8,128)(2,1)}), bf16[32,64,1024]{2,1,0:T(8,128)(2,1)}, u32[]{:S(2)}, u32[]{:S(2)}) async-start(bf16[32,64,1024]{2,1,0:T(8,128)(2,1)} %copy.66), calls=%async_computation.2 | async-start | bytes 8388608 | tf_op jit(solution)/shard_map/all_to_all | solution.py:46
  66.8 190.2 %reduce-scatter.2.cloned.1.call-start = ((), (), s32[]{:S(2)}) async-start(), calls=%async_computation.5 | async-start | bytes 4456448 | tf_op jit(solution)/shard_map/reduce_scatter | solution.py:56
  174.4 18.3 %all-to-all-start.3 = ((f32[32,1,4096]{2,1,0:T(1,128)}), f32[32,1,4096]{2,1,0:T(1,128)}, u32[]{:S(2)}, u32[]{:S(2)}) async-start(f32[32,1,4096]{2,1,0:T(1,128)} %reshape.88), calls=%async_computation.4 | async-start | bytes 1048576 | tf_op jit(solution)/shard_map/all_to_all | solution.py:86
  192.8 57.4 %all-to-all-start.2 = ((f32[32,512,64]{1,2,0:T(8,128)}), f32[32,512,64]{1,2,0:T(8,128)}, u32[]{:S(2)}, u32[]{:S(2)}) async-start(f32[32,512,64]{1,2,0:T(8,128)} %copy.71), calls=%async_computation.3 | async-start | bytes 8388608 | tf_op jit(solution)/shard_map/all_to_all | solution.py:85
  198.7 119.8 %all-gather.7.cloned.1.call-start = ((), (), s32[]{:S(2)}) async-start(), calls=%async_computation.7 | async-start | bytes 2228224 | tf_op jit(solution)/shard_map/all_gather | solution.py:93
  202.3 4.9 %copy-start.2 = (bf16[8,512,64]{1,0,2:T(8,128)(2,1)S(1)}, bf16[8,512,64]{1,0,2:T(8,128)(2,1)}, u32[]{:S(2)}) copy-start(bf16[8,512,64]{1,0,2:T(8,128)(2,1)} %copy-done.1) | copy-start | bytes 1572868
  206.7 1.6 copy-start.5
  206.7 1.9 copy-start.7
Sparse Core Ops, SparseCore 0:
  10.1 77.9 all-gather.4
  90.7 74.9 all-gather.8
  168.6 75.6 reduce-scatter.1
  246.8 71.7 all-gather.6
